TPU v7x, 32 devices: a whole 2x2x4 slice. The times are simulated.
32 devices in a mesh: groups: 2 (over y), latent: 4 (over z), rows: 4 (over x, core).
Axes of the slice: x: 2, y: 2, z: 4, core: 2. Of those that a mesh axis runs over, the one named last changes fastest.
Arguments:
- activations_in: bfloat16 [2, 128, 2304], P('groups', None, 'latent'), parts along dimension 0, may hold values from -6 to 6
- gate_proj: bfloat16 [2304, 4608], P('rows', 'latent'), may hold values from -0.125 to 0.125
- up_proj: bfloat16 [2304, 4608], P('rows', 'latent'), may hold values from -0.125 to 0.125
- down_proj: bfloat16 [4608, 2304], P('latent', 'rows'), may hold values from -0.09375 to 0.09375
- enc_weight: bfloat16 [4608, 65536], P(('groups', 'rows'), 'latent'), parts along dimension 0, may hold values from -6 to 6
- enc_bias: float32 [131072], P(('groups', 'latent')), parts along dimension 0, may hold values from -0.5 to 0.5
- dec_weight: bfloat16 [131072, 2304], P(('groups', 'latent'), 'rows'), parts along dimension 0, may hold values from -6 to 6
- dec_bias: float32 [4608], P(('groups', 'rows')), parts along dimension 0, may hold values from -0.5 to 0.5
Outputs:
- enc_weight_new: bfloat16 [4608, 65536], P(('groups', 'rows'), 'latent'), parts along dimension 0
- enc_bias_new: float32 [131072], P(('groups', 'latent')), parts along dimension 0
- dec_weight_new: bfloat16 [131072, 2304], P(('groups', 'latent'), 'rows'), parts along dimension 0
- dec_bias_new: float32 [4608], P(('groups', 'rows')), parts along dimension 0
There are 2 independent parts, one for each index of `groups`. A program takes and returns all parts, laid end to end along the dimension named above; an argument that names none is the same for every part. Nothing has to cross between parts.
All inputs are finite; a program needn't handle non-finite values.
Results may differ from a plain program's by a relative error of at most 0.02.
Values may be sent and summed in bfloat16 or wider, within the bound.
A program may use at most 128 MiB of HBM per device.

v0:
```python
import jax
import jax.numpy as jnp
from jax import lax
from jax.sharding import PartitionSpec as P

MODEL_WIDTH = 2304
LATENTS = 65536
sparsity_cost = 0.1
sharpness = 8.0
weight_rate = 2.0
enc_bias_rate = 0.01
dec_bias_rate = 0.002


def row_total(term):
    return lax.psum(term.astype(jnp.bfloat16), "rows").astype(jnp.float32)


def body(activations_in, gate_proj, up_proj, down_proj, enc_weight, enc_bias, dec_weight, dec_bias):
    gate_full, up_full = (
        lax.all_gather(gate_proj, "rows", axis=0, tiled=True),
        lax.all_gather(up_proj, "rows", axis=0, tiled=True),
    )
    batches = activations_in.shape[0]
    batch_tokens = activations_in.shape[1]
    all_tokens = batches * batch_tokens
    token_rows = activations_in.reshape(all_tokens, activations_in.shape[2])
    portion = lax.all_gather(token_rows, "latent", axis=1, tiled=True)
    gate_term = jnp.dot(portion, gate_full, preferred_element_type=jnp.float32)
    up_term = jnp.dot(portion, up_full, preferred_element_type=jnp.float32)
    hidden = (jax.nn.gelu(gate_term, approximate=True) * up_term).astype(jnp.bfloat16)
    partial_value = jnp.dot(hidden, down_proj, preferred_element_type=jnp.float32)
    features = lax.psum(partial_value, "latent").astype(jnp.bfloat16)
    features = features.reshape(batches, batch_tokens, features.shape[1])
    enc_scale = MODEL_WIDTH ** (-0.5)
    dec_scale = LATENTS ** (-0.5)
    inputs = features[0]
    local_pre = jnp.dot(inputs, enc_weight, preferred_element_type=jnp.float32)
    pre_latent = enc_scale * row_total(local_pre) + enc_bias
    latents = (jax.nn.softplus(sharpness * pre_latent) / sharpness).astype(jnp.bfloat16)
    local_rebuilt = jnp.dot(latents, dec_weight, preferred_element_type=jnp.float32)
    rebuilt_share = lax.psum_scatter(local_rebuilt, "latent", scatter_dimension=1, tiled=True)
    share_cols = rebuilt_share.shape[1]
    col_offset = lax.axis_index("latent") * share_cols
    inputs_here = lax.dynamic_slice_in_dim(inputs, col_offset, share_cols, 1)
    bias_here = lax.dynamic_slice_in_dim(dec_bias, col_offset, share_cols, 0)
    grad_share = (
        2.0 * (dec_scale * rebuilt_share + bias_here - inputs_here.astype(jnp.float32))
    ).astype(jnp.bfloat16)
    residual_grad = lax.all_gather(grad_share, "latent", axis=1, tiled=True)
    local_back = lax.dot_general(
        residual_grad, dec_weight, (((1,), (1,)), ((), ())), preferred_element_type=jnp.float32
    )
    back_sum = row_total(local_back)
    latent_grad = (
        jax.nn.sigmoid(sharpness * pre_latent) * (dec_scale * back_sum + sparsity_cost)
    ).astype(jnp.bfloat16)
    dec_grad = dec_scale * lax.dot_general(
        latents, residual_grad, (((0,), (0,)), ((), ())), preferred_element_type=jnp.float32
    )
    enc_grad = enc_scale * lax.dot_general(
        inputs, latent_grad, (((0,), (0,)), ((), ())), preferred_element_type=jnp.float32
    )
    enc_bias = enc_bias - enc_bias_rate * jnp.sum(latent_grad, axis=0, dtype=jnp.float32)
    dec_bias = dec_bias - dec_bias_rate * jnp.sum(residual_grad, axis=0, dtype=jnp.float32)
    enc_weight = (enc_weight.astype(jnp.float32) - weight_rate * enc_grad).astype(jnp.bfloat16)
    dec_weight = (dec_weight.astype(jnp.float32) - weight_rate * dec_grad).astype(jnp.bfloat16)
    return (enc_weight, enc_bias, dec_weight, dec_bias)


def solution(mesh):
    return jax.shard_map(
        body,
        mesh=mesh,
        in_specs=(
            P("groups", None, "latent"),
            P("rows", "latent"),
            P("rows", "latent"),
            P("latent", "rows"),
            P(("groups", "rows"), "latent"),
            P(("groups", "latent")),
            P(("groups", "latent"), "rows"),
            P(("groups", "rows")),
        ),
        out_specs=(
            P(("groups", "rows"), "latent"),
            P(("groups", "latent")),
            P(("groups", "latent"), "rows"),
            P(("groups", "rows")),
        ),
        check_vma=False,
    )
```

profile of v0, /device:TPU:0, one launch (start us, length us, event | category | flops | bytes accessed | tf_op | source)
XLA Modules:
  0.0 395.9 jit_solution(4908214912626969955)
XLA Ops:
  7.2 0.0 copy-start
  7.2 0.0 all-gather.4.cloned.1.call-start
  7.2 0.7 all-gather.4.cloned.1.call-update
  7.9 0.0 all-gather.6.cloned.1.call-start
  8.0 0.7 all-gather.6.cloned.1.call-update
  8.7 0.0 all-reduce.4.cloned.1.call-start
  8.7 18.5 %all-gather = bf16[1,128,2304]{1,2,0:T(8,128)(2,1)S(1)} all-gather(bf16[1,128,576]{1,2,0:T(8,128)(2,1)} %param.8), channel_id=2, replica_groups=mesh['groups'=2,'latent'=4,'rows'=4] {'latent'}, dimensions={2}, use_global_device_ids=true | all-gather | bytes 737280 | tf_op jit(solution)/shard_map/all_gather | solution.py:28
  27.2 25.9 %all-gather.4.cloned.1.call-done = bf16[2304,1152]{1,0:T(8,128)(2,1)} async-done(((bf16[576,1152]{1,0:T(8,128)(2,1)}), bf16[2304,1152]{1,0:T(8,128)(2,1)}) %all-gather.4.cloned.1.call-update) | async-done | bytes 5308432 | tf_op jit(solution)/shard_map/all_gather | solution.py:21
  53.1 3.5 fusion.14
  56.6 38.9 %all-gather.6.cloned.1.call-done = bf16[2304,1152]{1,0:T(8,128)(2,1)} async-done(((bf16[576,1152]{1,0:T(8,128)(2,1)}), bf16[2304,1152]{1,0:T(8,128)(2,1)}) %all-gather.6.cloned.1.call-update) | async-done | bytes 5308432 | tf_op jit(solution)/shard_map/all_gather | solution.py:22
  95.5 0.0 copy-done
  95.5 4.0 fusion.3
  99.4 25.3 %all-reduce.7 = bf16[128,576]{0,1:T(8,128)(2,1)S(1)} all-reduce(f32[128,576]{0,1:T(8,128)S(1)} %fusion.3), channel_id=1, replica_groups=mesh['groups'=2,'latent'=4,'rows'=4] {'latent'}, use_global_device_ids=true, to_apply=%region_0.0 | all-reduce | flops 73728 | bytes 442368 | tf_op jit(solution)/shard_map/psum | solution.py:33
  124.7 0.0 copy-start.2
  124.8 12.0 %convolution_convert_fusion.1 = bf16[128,16384]{1,0:T(8,128)(2,1)} fusion(bf16[128,576]{0,1:T(8,128)(2,1)S(1)} %all-reduce.7, bf16[576,16384]{1,0:T(8,128)(2,1)} %param.12), kind=kOutput, calls=%fused_computation.4 | convolution fusion | flops 2418016256 | bytes 23216128 | tf_op jit(solution)/shard_map/dot_general | solution.py:38
  136.7 0.0 all-reduce.4.cloned.1.call-update
  136.8 0.0 copy-start.3
  136.8 0.2 reduce-scatter.2.cloned.1.call-start
  137.0 82.7 %all-reduce.4.cloned.1.call-done = bf16[128,16384]{1,0:T(8,128)(2,1)} async-done(((bf16[128,16384]{1,0:T(8,128)(2,1)}), bf16[128,16384]{1,0:T(8,128)(2,1)}) %all-reduce.4.cloned.1.call-update) | async-done | bytes 4194320 | tf_op jit(solution)/shard_map/psum | solution.py:16
  219.7 0.0 copy-done.2
  219.7 15.9 %fusion.25 = f32[128,576]{0,1:T(8,128)} fusion(bf16[16384,576]{0,1:T(8,128)(2,1)} %param.14, bf16[128,16384]{1,0:T(8,128)(2,1)} %all-reduce.4.cloned.1.call-done, f32[16384]{0:T(1024)S(1)} %copy-done.2), kind=kOutput, calls=%fused_computation.36 | convolution fusion | flops 2441084928 | bytes 23429120 | tf_op jit(solution)/shard_map/dot_general | solution.py:41
  235.6 0.0 reduce-scatter.2.cloned.1.call-update
  235.6 0.0 all-reduce.6.cloned.1.call-start
  235.7 0.0 copy-done.3
  235.7 0.1 dynamic_slice.6
  235.8 20.4 %reduce-scatter.2.cloned.1.call-done = f32[128,144]{0,1:T(8,128)} async-done(((f32[128,576]{0,1:T(8,128)}), f32[128,144]{0,1:T(8,128)}) %reduce-scatter.2.cloned.1.call-update) | async-done | bytes 73744 | tf_op jit(solution)/shard_map/reduce_scatter | solution.py:42
  256.2 1.0 multiply_convert_fusion.1
  257.1 13.5 %all_gather.15 = bf16[128,576]{0,1:T(8,128)(2,1)S(1)} all-gather(bf16[128,144]{0,1:T(8,128)(2,1)S(1)} %multiply_convert_fusion.1), channel_id=1, replica_groups=mesh['groups'=2,'latent'=4,'rows'=4] {'latent'}, dimensions={1}, use_global_device_ids=true | all-gather | bytes 184320 | tf_op jit(solution)/shard_map/all_gather | solution.py:50
  270.6 12.0 %convolution_convert_fusion = bf16[128,16384]{1,0:T(8,128)(2,1)} fusion(bf16[128,576]{0,1:T(8,128)(2,1)S(1)} %all_gather.15, bf16[16384,576]{0,1:T(8,128)(2,1)} %param.14), kind=kOutput, calls=%fused_computation.3 | convolution fusion | flops 2418016256 | bytes 23216128 | tf_op jit(solution)/shard_map/dot_general | solution.py:51
  282.6 0.1 convert_reduce_fusion.1
  282.7 0.0 all-reduce.6.cloned.1.call-update
  282.7 0.6 multiply_subtract_fusion.1
  283.3 32.5 %subtract_convert_fusion = bf16[16384,576]{0,1:T(8,128)(2,1)} fusion(bf16[16384,576]{0,1:T(8,128)(2,1)} %param.14, bf16[128,576]{0,1:T(8,128)(2,1)S(1)} %all_gather.15, bf16[128,16384]{1,0:T(8,128)(2,1)} %all-reduce.4.cloned.1.call-done, f32[16384]{0:T(1024)S(1)} %copy-done.2), kind=kOutput, calls=%fused_computation | convolution fusion | flops 2478833664 | bytes 42156032 | tf_op jit(solution)/shard_map/dot_general | solution.py:58
  315.8 50.7 %all-reduce.6.cloned.1.call-done = bf16[128,16384]{1,0:T(8,128)(2,1)} async-done(((bf16[128,16384]{1,0:T(8,128)(2,1)}), bf16[128,16384]{1,0:T(8,128)(2,1)}) %all-reduce.6.cloned.1.call-update) | async-done | bytes 4194320 | tf_op jit(solution)/shard_map/psum | solution.py:16
  366.5 7.7 %convert_reduce_fusion = (f32[16384]{0:T(1024)S(1)}, bf16[128,16384]{1,0:T(8,128)(2,1)}) fusion(bf16[128,16384]{1,0:T(8,128)(2,1)} %all-reduce.6.cloned.1.call-done, f32[16384]{0:T(1024)S(1)} %copy-done.2, bf16[128,16384]{1,0:T(8,128)(2,1)} %all-reduce.4.cloned.1.call-done), kind=kLoop, calls=%fused_computation.7 | loop fusion | flops 29343744 | bytes 12713984 | tf_op jit(solution)/shard_map/reduce_sum | solution.py:64
  374.2 0.0 copy-start.1
  374.2 14.5 %subtract_convert_fusion.1 = bf16[576,16384]{1,0:T(8,128)(2,1)} fusion(bf16[576,16384]{1,0:T(8,128)(2,1)} %param.12, bf16[128,576]{0,1:T(8,128)(2,1)S(1)} %all-reduce.7, bf16[128,16384]{1,0:T(8,128)(2,1)} %get-tuple-element.5), kind=kOutput, calls=%fused_computation.1 | convolution fusion | flops 2453667840 | bytes 42090496 | tf_op jit(solution)/shard_map/dot_general | solution.py:61
  388.7 0.6 multiply_subtract_fusion
  389.3 0.0 copy-done.1
Async XLA Ops:
  7.2 88.3 %copy-start = (bf16[1152,576]{0,1:T(8,128)(2,1)S(1)}, bf16[1152,576]{0,1:T(8,128)(2,1)}, u32[]{:S(2)}) copy-start(bf16[1152,576]{0,1:T(8,128)(2,1)} %param.11) | copy-start | bytes 3981316
  7.2 45.9 %all-gather.4.cloned.1.call-start = ((), (), s32[]{:S(2)}) async-start(), calls=%async_computation.1 | async-start | bytes 6635520 | tf_op jit(solution)/shard_map/all_gather | solution.py:21
  7.9 87.5 %all-gather.6.cloned.1.call-start = ((), (), s32[]{:S(2)}) async-start(), calls=%async_computation.2 | async-start | bytes 6635520 | tf_op jit(solution)/shard_map/all_gather | solution.py:22
  8.7 211.0 %all-reduce.4.cloned.1.call-start = ((), (), s32[]{:S(2)}) async-start(), calls=%async_computation.3 | async-start | bytes 8388608 | tf_op jit(solution)/shard_map/psum | solution.py:16
  124.7 94.9 %copy-start.2 = (f32[16384]{0:T(1024)S(1)}, f32[16384]{0:T(1024)}, u32[]{:S(2)}) copy-start(f32[16384]{0:T(1024)} %param.13) | copy-start | bytes 196612
  136.8 98.9 %copy-start.3 = (f32[576]{0:T(1024)S(1)}, f32[576]{0:T(1024)}, u32[]{:S(2)}) copy-start(f32[576]{0:T(1024)} %param.15) | copy-start | bytes 6916
  136.8 119.4 %reduce-scatter.2.cloned.1.call-start = ((), (), s32[]{:S(2)}) async-start(), calls=%async_computation.4 | async-start | bytes 368640 | tf_op jit(solution)/shard_map/reduce_scatter | solution.py:42
  235.6 130.9 %all-reduce.6.cloned.1.call-start = ((), (), s32[]{:S(2)}) async-start(), calls=%async_computation.5 | async-start | bytes 8388608 | tf_op jit(solution)/shard_map/psum | solution.py:16
  374.2 15.1 %copy-start.1 = (bf16[1152,576]{0,1:T(8,128)(2,1)S(1)}, bf16[1152,576]{0,1:T(8,128)(2,1)}, u32[]{:S(2)}) copy-start(bf16[1152,576]{0,1:T(8,128)(2,1)} %param.11) | copy-start | bytes 3981316
Sparse Core Ops, SparseCore 0:
  9.5 43.4 all-gather.3
  54.6 40.7 all-gather.5
  136.9 82.7 all-reduce.3
  235.8 20.3 reduce-scatter.1
  282.9 83.6 all-reduce.5
where the time goes:
time: 396 us
  waiting for transfers between devices  220 us (56%)
  matrix products  94.3 us (24%)
  blocking collectives  57.3 us (14%)
  between operations  13.8 us (3%)
  other arithmetic  10 us (3%)
    psum x2, waiting for transfers between devices, row_total(): return lax.psum(term.astype(jnp.bfloat16), 'rows').astype(jnp.float32)  133 us
    all_gather x1, waiting for transfers between devices, body(): lax.all_gather(up_proj, 'rows', axis=0, tiled=True)  38.9 us
    dot_general x1, matrix products, body(): lax.dot_general(latents, residual_grad, (((0,), (0,)), ((), ())), preferr...  32.5 us
    all_gather x1, waiting for transfers between devices, body(): lax.all_gather(gate_proj, 'rows', axis=0, tiled=True)  25.9 us
    psum x1, blocking collectives, body(): features = lax.psum(partial_value, 'latent').astype(jnp.bfloat16)  25.3 us
    reduce_scatter x1, waiting for transfers between devices, body(): lax.psum_scatter(local_rebuilt, 'latent', scatter_dimension=1, tiled=True)  20.4 us
    all_gather x1, blocking collectives, body(): portion = lax.all_gather(token_rows, 'latent', axis=1, tiled=True)  18.5 us
    dot_general x1, matrix products, body(): jnp.dot(latents, dec_weight, preferred_element_type=jnp.float32)  15.9 us
  transfers between devices with their start and end apart: 5, of which 5 were waited for; matrix products, arithmetic and copies ran while one was open for 9% of the time, Pallas kernels for 0%

commit v1 on v0

--- a/solution.py
+++ b/solution.py
@@ -10,6 +10,12 @@
 weight_rate = 2.0
 enc_bias_rate = 0.01
 dec_bias_rate = 0.002
+
+
+def add_all(x, axis):
+    blocks = lax.all_gather(x, axis, axis=0, tiled=False)
+    total = blocks.sum(axis=0)
+    return total
 
 
 def row_total(term):
@@ -30,7 +36,7 @@
     up_term = jnp.dot(portion, up_full, preferred_element_type=jnp.float32)
     hidden = (jax.nn.gelu(gate_term, approximate=True) * up_term).astype(jnp.bfloat16)
     partial_value = jnp.dot(hidden, down_proj, preferred_element_type=jnp.float32)
-    features = lax.psum(partial_value, "latent").astype(jnp.bfloat16)
+    features = add_all(partial_value, "latent").astype(jnp.bfloat16)
     features = features.reshape(batches, batch_tokens, features.shape[1])
     enc_scale = MODEL_WIDTH ** (-0.5)
     dec_scale = LATENTS ** (-0.5)

time: 396 us -> 407 us (1.028)
  waiting for transfers between devices: 220 us -> 253 us
  blocking collectives: 57.3 us -> 32 us
    all_gather x0 -> x1, waiting for transfers between devices: none -> 31.8 us  [add_all(): blocks = lax.all_gather(x, axis, axis=0, tiled=False)]
    psum x1 -> x0, blocking collectives: 25.3 us -> none  [body(): features = lax.psum(partial_value, 'latent').astype(jnp.bfloat16)]
  transfers between devices with their start and end apart: 5 -> 6, of which waited for: 5 -> 6; matrix products, arithmetic and copies ran while one was open for 9% -> 9% of each run, Pallas kernels for 0% -> 0%
where the time goes in v1:
time: 407 us
  waiting for transfers between devices  253 us (62%)
  matrix products  95 us (23%)
  blocking collectives  32 us (8%)
  between operations  14.2 us (3%)
  other arithmetic  10.7 us (3%)
    psum x2, waiting for transfers between devices, row_total(): return lax.psum(term.astype(jnp.bfloat16), 'rows').astype(jnp.float32)  134 us
    all_gather x1, waiting for transfers between devices, body(): lax.all_gather(up_proj, 'rows', axis=0, tiled=True)  38.9 us
    dot_general x1, matrix products, body(): lax.dot_general(latents, residual_grad, (((0,), (0,)), ((), ())), preferr...  32.5 us
    all_gather x1, waiting for transfers between devices, add_all(): blocks = lax.all_gather(x, axis, axis=0, tiled=False)  31.8 us
    all_gather x1, waiting for transfers between devices, body(): lax.all_gather(gate_proj, 'rows', axis=0, tiled=True)  25.9 us
    reduce_scatter x1, waiting for transfers between devices, body(): lax.psum_scatter(local_rebuilt, 'latent', scatter_dimension=1, tiled=True)  20.4 us
    all_gather x1, blocking collectives, body(): portion = lax.all_gather(token_rows, 'latent', axis=1, tiled=True)  18.5 us
    dot_general x1, matrix products, body(): jnp.dot(latents, dec_weight, preferred_element_type=jnp.float32)  15.9 us
  transfers between devices with their start and end apart: 6, of which 6 were waited for; matrix products, arithmetic and copies ran while one was open for 9% of the time, Pallas kernels for 0%

profile of v1, /device:TPU:0, one launch (start us, length us, event | category | flops | bytes accessed | tf_op | source)
XLA Modules:
  0.0 406.9 jit_solution(7723960838168735028)
XLA Ops:
  7.2 0.0 copy-start
  7.2 0.0 all-gather.6.cloned.1.call-start
  7.2 0.7 all-gather.6.cloned.1.call-update
  7.9 0.0 all-gather.8.cloned.1.call-start
  8.0 0.7 all-gather.8.cloned.1.call-update
  8.7 0.0 all-gather.10.cloned.1.call-start
  8.7 18.5 %all-gather = bf16[1,128,2304]{1,2,0:T(8,128)(2,1)S(1)} all-gather(bf16[1,128,576]{1,2,0:T(8,128)(2,1)} %param.8), channel_id=2, replica_groups=mesh['groups'=2,'latent'=4,'rows'=4] {'latent'}, dimensions={2}, use_global_device_ids=true | all-gather | bytes 737280 | tf_op jit(solution)/shard_map/all_gather | solution.py:34
  27.2 25.9 %all-gather.6.cloned.1.call-done = bf16[2304,1152]{1,0:T(8,128)(2,1)} async-done(((bf16[576,1152]{1,0:T(8,128)(2,1)}), bf16[2304,1152]{1,0:T(8,128)(2,1)}) %all-gather.6.cloned.1.call-update) | async-done | bytes 5308432 | tf_op jit(solution)/shard_map/all_gather | solution.py:27
  53.1 3.5 fusion.14
  56.6 38.9 %all-gather.8.cloned.1.call-done = bf16[2304,1152]{1,0:T(8,128)(2,1)} async-done(((bf16[576,1152]{1,0:T(8,128)(2,1)}), bf16[2304,1152]{1,0:T(8,128)(2,1)}) %all-gather.8.cloned.1.call-update) | async-done | bytes 5308432 | tf_op jit(solution)/shard_map/all_gather | solution.py:28
  95.5 0.0 copy-done
  95.5 4.7 %fusion.3 = f32[128,576]{0,1:T(8,128)} fusion(bf16[1152,576]{0,1:T(8,128)(2,1)S(1)} %copy-done, bf16[2304,1152]{1,0:T(8,128)(2,1)} %all-gather.8.cloned.1.call-done, f32[128,1152]{1,0:T(8,128)S(1)} %fusion.14, bf16[1,128,2304]{1,2,0:T(8,128)(2,1)S(1)} %all-gather), kind=kOutput, calls=%fused_computation.12 | convolution fusion | flops 850821120 | bytes 8110080 | tf_op jit(solution)/shard_map/dot_general | solution.py:38
  100.1 0.0 all-gather.10.cloned.1.call-update
  100.2 0.0 all-reduce.3.cloned.1.call-start
  100.2 31.8 %all-gather.10.cloned.1.call-done = f32[512,576]{0,1:T(8,128)} async-done(((f32[128,576]{0,1:T(8,128)}), f32[512,576]{0,1:T(8,128)}) %all-gather.10.cloned.1.call-update) | async-done | bytes 1179664 | tf_op jit(solution)/shard_map/all_gather | solution.py:16
  132.0 1.7 reshape.15
  133.7 0.8 reduce_sum.27
  134.5 0.0 copy-start.2
  134.5 12.0 %convolution_convert_fusion.1 = bf16[128,16384]{1,0:T(8,128)(2,1)} fusion(bf16[128,576]{0,1:T(8,128)(2,1)S(1)} %reduce_sum.27, bf16[576,16384]{1,0:T(8,128)(2,1)} %param.12), kind=kOutput, calls=%fused_computation.4 | convolution fusion | flops 2418016256 | bytes 23216128 | tf_op jit(solution)/shard_map/dot_general | solution.py:44
  146.4 0.0 all-reduce.3.cloned.1.call-update
  146.5 0.0 copy-start.3
  146.5 0.2 reduce-scatter.2.cloned.1.call-start
  146.7 83.7 %all-reduce.3.cloned.1.call-done = bf16[128,16384]{1,0:T(8,128)(2,1)} async-done(((bf16[128,16384]{1,0:T(8,128)(2,1)}), bf16[128,16384]{1,0:T(8,128)(2,1)}) %all-reduce.3.cloned.1.call-update) | async-done | bytes 4194320 | tf_op jit(solution)/shard_map/psum | solution.py:22
  230.5 0.0 copy-done.2
  230.5 15.9 %fusion.25 = f32[128,576]{0,1:T(8,128)} fusion(bf16[16384,576]{0,1:T(8,128)(2,1)} %param.14, bf16[128,16384]{1,0:T(8,128)(2,1)} %all-reduce.3.cloned.1.call-done, f32[16384]{0:T(1024)S(1)} %copy-done.2), kind=kOutput, calls=%fused_computation.36 | convolution fusion | flops 2441084928 | bytes 23429120 | tf_op jit(solution)/shard_map/dot_general | solution.py:47
  246.4 0.0 reduce-scatter.2.cloned.1.call-update
  246.4 0.0 all-reduce.5.cloned.1.call-start
  246.5 0.0 copy-done.3
  246.5 0.1 dynamic_slice.6
  246.5 20.4 %reduce-scatter.2.cloned.1.call-done = f32[128,144]{0,1:T(8,128)} async-done(((f32[128,576]{0,1:T(8,128)}), f32[128,144]{0,1:T(8,128)}) %reduce-scatter.2.cloned.1.call-update) | async-done | bytes 73744 | tf_op jit(solution)/shard_map/reduce_scatter | solution.py:48
  266.9 1.0 multiply_convert_fusion.1
  267.9 13.5 %all_gather.23 = bf16[128,576]{0,1:T(8,128)(2,1)S(1)} all-gather(bf16[128,144]{0,1:T(8,128)(2,1)S(1)} %multiply_convert_fusion.1), channel_id=1, replica_groups=mesh['groups'=2,'latent'=4,'rows'=4] {'latent'}, dimensions={1}, use_global_device_ids=true | all-gather | bytes 184320 | tf_op jit(solution)/shard_map/all_gather | solution.py:56
  281.4 12.0 %convolution_convert_fusion = bf16[128,16384]{1,0:T(8,128)(2,1)} fusion(bf16[128,576]{0,1:T(8,128)(2,1)S(1)} %all_gather.23, bf16[16384,576]{0,1:T(8,128)(2,1)} %param.14), kind=kOutput, calls=%fused_computation.3 | convolution fusion | flops 2418016256 | bytes 23216128 | tf_op jit(solution)/shard_map/dot_general | solution.py:57
  293.3 0.1 convert_reduce_fusion.1
  293.5 0.0 all-reduce.5.cloned.1.call-update
  293.5 0.6 multiply_subtract_fusion.1
  294.1 32.5 %subtract_convert_fusion = bf16[16384,576]{0,1:T(8,128)(2,1)} fusion(bf16[16384,576]{0,1:T(8,128)(2,1)} %param.14, bf16[128,576]{0,1:T(8,128)(2,1)S(1)} %all_gather.23, bf16[128,16384]{1,0:T(8,128)(2,1)} %all-reduce.3.cloned.1.call-done, f32[16384]{0:T(1024)S(1)} %copy-done.2), kind=kOutput, calls=%fused_computation | convolution fusion | flops 2478833664 | bytes 42156032 | tf_op jit(solution)/shard_map/dot_general | solution.py:64
  326.6 50.7 %all-reduce.5.cloned.1.call-done = bf16[128,16384]{1,0:T(8,128)(2,1)} async-done(((bf16[128,16384]{1,0:T(8,128)(2,1)}), bf16[128,16384]{1,0:T(8,128)(2,1)}) %all-reduce.5.cloned.1.call-update) | async-done | bytes 4194320 | tf_op jit(solution)/shard_map/psum | solution.py:22
  377.3 7.6 %convert_reduce_fusion = (f32[16384]{0:T(1024)S(1)}, bf16[128,16384]{1,0:T(8,128)(2,1)}) fusion(bf16[128,16384]{1,0:T(8,128)(2,1)} %all-reduce.5.cloned.1.call-done, f32[16384]{0:T(1024)S(1)} %copy-done.2, bf16[128,16384]{1,0:T(8,128)(2,1)} %all-reduce.3.cloned.1.call-done), kind=kLoop, calls=%fused_computation.7 | loop fusion | flops 29343744 | bytes 12713984 | tf_op jit(solution)/shard_map/reduce_sum | solution.py:70
  384.9 0.0 copy-start.1
  384.9 14.5 %subtract_convert_fusion.1 = bf16[576,16384]{1,0:T(8,128)(2,1)} fusion(bf16[576,16384]{1,0:T(8,128)(2,1)} %param.12, bf16[128,576]{0,1:T(8,128)(2,1)S(1)} %reduce_sum.27, bf16[128,16384]{1,0:T(8,128)(2,1)} %get-tuple-element.5), kind=kOutput, calls=%fused_computation.1 | convolution fusion | flops 2453667840 | bytes 42090496 | tf_op jit(solution)/shard_map/dot_general | solution.py:67
  399.4 0.6 multiply_subtract_fusion
  400.0 0.0 copy-done.1
Async XLA Ops:
  7.2 88.3 %copy-start = (bf16[1152,576]{0,1:T(8,128)(2,1)S(1)}, bf16[1152,576]{0,1:T(8,128)(2,1)}, u32[]{:S(2)}) copy-start(bf16[1152,576]{0,1:T(8,128)(2,1)} %param.11) | copy-start | bytes 3981316
  7.2 45.9 %all-gather.6.cloned.1.call-start = ((), (), s32[]{:S(2)}) async-start(), calls=%async_computation.1 | async-start | bytes 6635520 | tf_op jit(solution)/shard_map/all_gather | solution.py:27
  7.9 87.5 %all-gather.8.cloned.1.call-start = ((), (), s32[]{:S(2)}) async-start(), calls=%async_computation.2 | async-start | bytes 6635520 | tf_op jit(solution)/shard_map/all_gather | solution.py:28
  8.7 123.4 %all-gather.10.cloned.1.call-start = ((), (), s32[]{:S(2)}) async-start(), calls=%async_computation.6 | async-start | bytes 1474560 | tf_op jit(solution)/shard_map/all_gather | solution.py:16
  100.2 130.3 %all-reduce.3.cloned.1.call-start = ((), (), s32[]{:S(2)}) async-start(), calls=%async_computation.3 | async-start | bytes 8388608 | tf_op jit(solution)/shard_map/psum | solution.py:22
  134.5 96.0 %copy-start.2 = (f32[16384]{0:T(1024)S(1)}, f32[16384]{0:T(1024)}, u32[]{:S(2)}) copy-start(f32[16384]{0:T(1024)} %param.13) | copy-start | bytes 196612
  146.5 100.0 %copy-start.3 = (f32[576]{0:T(1024)S(1)}, f32[576]{0:T(1024)}, u32[]{:S(2)}) copy-start(f32[576]{0:T(1024)} %param.15) | copy-start | bytes 6916
  146.5 120.4 %reduce-scatter.2.cloned.1.call-start = ((), (), s32[]{:S(2)}) async-start(), calls=%async_computation.4 | async-start | bytes 368640 | tf_op jit(solution)/shard_map/reduce_scatter | solution.py:48
  246.4 130.9 %all-reduce.5.cloned.1.call-start = ((), (), s32[]{:S(2)}) async-start(), calls=%async_computation.5 | async-start | bytes 8388608 | tf_op jit(solution)/shard_map/psum | solution.py:22
  384.9 15.1 %copy-start.1 = (bf16[1152,576]{0,1:T(8,128)(2,1)S(1)}, bf16[1152,576]{0,1:T(8,128)(2,1)}, u32[]{:S(2)}) copy-start(bf16[1152,576]{0,1:T(8,128)(2,1)} %param.11) | copy-start | bytes 3981316
Sparse Core Ops, SparseCore 0:
  9.5 43.4 all-gather.5
  54.6 40.7 all-gather.7
  100.3 31.7 all-gather.9
  146.6 83.8 all-reduce.2
  246.5 20.3 reduce-scatter.1
  293.6 83.6 all-reduce.4
